TPU v7x, 32 devices: a whole 2x2x4 slice. The times are simulated.
32 devices in a mesh: dp: 8 (over z, x), fsdp: 4 (over y, core).
Axes of the slice: x: 2, y: 2, z: 4, core: 2. Of those that a mesh axis runs over, the one named last changes fastest.
Arguments:
- acts: bfloat16 [1024, 3072], P('dp'), may hold values from -6 to 6
- weight: bfloat16 [3072, 3072], P('dp', 'fsdp'), may hold values from -0.15625 to 0.15625
- block_mask: int32 [4, 12, 12], replicated, may hold values 0 or 1
- out_grad: bfloat16 [4, 1024, 3072], P(None, 'dp', 'fsdp'), may hold values from -6 to 6
Outputs:
- outputs: bfloat16 [4, 1024, 3072], P(None, 'dp', 'fsdp')
- grad_w: float32 [3072, 3072], P('dp', 'fsdp')
- grad_x: bfloat16 [1024, 3072], P('dp', 'fsdp')
All inputs are finite; a program needn't handle non-finite values.
Results may differ from a plain program's by a relative error of at most 0.001.
Values may be sent and summed in bfloat16 or wider, within the bound.
No kernel may reach another device: no remote copies, remote signals or barrier semaphores. Data moves between devices by JAX's collectives and lax.ppermute only.
A program may use at most 128 MiB of HBM per device.

v0:
```python
import jax
import jax.numpy as jnp
from jax import lax
from jax.sharding import PartitionSpec as P

BS = 256
TOK_G = 128


def on_device(acts, weight, block_mask, out_grad):
    width = weight.shape[1]
    kblocks = block_mask.shape[1]
    oblocks = block_mask.shape[2]
    first_col = lax.axis_index("fsdp") * width
    col_ids = (first_col + jnp.arange(width, dtype=jnp.int32)) // BS
    col_select = (col_ids[None, :] == jnp.arange(oblocks, dtype=jnp.int32)[:, None]).astype(
        jnp.float32
    )
    col_mask = jnp.einsum("skb,bc->skc", block_mask.astype(jnp.float32), col_select)

    def piece_mask(count):
        row_ids = jnp.arange(count, dtype=jnp.int32) // BS
        row_select = (row_ids[:, None] == jnp.arange(kblocks, dtype=jnp.int32)[None, :]).astype(
            jnp.float32
        )
        return jnp.einsum("nk,skc->snc", row_select, col_mask)

    def masked_piece(piece):
        return piece_mask(piece.shape[0]).astype(jnp.bfloat16) * piece[None]

    cols = acts
    forward = jnp.einsum(
        "tn,snc->stc",
        cols,
        masked_piece(lax.all_gather(weight, "dp", axis=0, tiled=True)),
        preferred_element_type=jnp.float32,
    )
    input_part = jnp.einsum(
        "stc,snc->tn",
        out_grad,
        masked_piece(lax.all_gather(weight, "dp", axis=0, tiled=True)),
        preferred_element_type=jnp.float32,
    )
    outputs = forward.astype(jnp.bfloat16)
    cols = acts
    products = jnp.einsum("tn,stc->snc", cols, out_grad, preferred_element_type=jnp.float32)
    grad_w = lax.psum_scatter(
        jnp.sum(piece_mask(lax.axis_size("dp") * weight.shape[0]) * products, axis=0)
        * (1.0 / TOK_G),
        "dp",
        scatter_dimension=0,
        tiled=True,
    )
    grad_x = lax.psum_scatter(input_part, "fsdp", scatter_dimension=1, tiled=True).astype(
        jnp.bfloat16
    )
    return (outputs, grad_w, grad_x)


def solution(mesh):
    in_specs = (P("dp", None), P("dp", "fsdp"), P(), P(None, "dp", "fsdp"))
    out_specs = (P(None, "dp", "fsdp"), P("dp", "fsdp"), P("dp", "fsdp"))
    return jax.shard_map(
        on_device, mesh=mesh, in_specs=in_specs, out_specs=out_specs, check_vma=False
    )
```

profile of v0, /device:TPU:0, one launch (start us, length us, event | category | flops | bytes accessed | tf_op | source)
XLA Modules:
  0.0 319.4 jit_solution(12060055116255987593)
XLA Ops:
  7.2 0.0 copy-start
  7.2 0.0 all-gather.2.cloned.1.call-start
  7.2 0.7 all-gather.2.cloned.1.call-update
  7.9 0.0 reduce-scatter.5.cloned.1.call-start
  8.0 0.7 convert_element_type.23
  8.7 15.5 %fusion.5 = f32[4,768,3072]{2,1,0:T(8,128)} fusion(s32[3072]{0:T(1024)S(1)} %add_select_fusion, bf16[4,12,12]{2,0,1:T(4,128)(2,1)S(1)} %convert_element_type.23, s32[768]{0:T(1024)S(1)} %add_select_fusion.1), kind=kOutput, calls=%fused_computation.9 | convolution fusion | flops 227423232 | bytes 37765248 | tf_op jit(solution)/shard_map/nk,skc->snc/dot_general | solution.py:26
  24.2 68.6 %all-gather.2.cloned.1.call-done = bf16[3072,768]{1,0:T(8,128)(2,1)} async-done(((bf16[384,768]{1,0:T(8,128)(2,1)}), bf16[3072,768]{1,0:T(8,128)(2,1)}) %all-gather.2.cloned.1.call-update) | async-done | bytes 4718608 | tf_op jit(solution)/shard_map/all_gather | solution.py:35
  92.8 6.6 %copy.12 = bf16[3072,768]{0,1:T(8,128)(2,1)} copy(bf16[3072,768]{1,0:T(8,128)(2,1)} %all-gather.2.cloned.1.call-done) | data formatting | bytes 9437184 | tf_op jit(solution)/shard_map/all_gather | solution.py:35
  99.5 0.0 copy-done
  99.5 0.0 copy-start.1
  99.5 16.7 %fusion.2 = f32[128,3072]{0,1:T(8,128)} fusion(bf16[4,128,768]{2,1,0:T(8,128)(2,1)S(1)} %copy-done, f32[4,768,3072]{2,1,0:T(8,128)} %fusion.5, bf16[3072,768]{0,1:T(8,128)(2,1)} %copy.12), kind=kOutput, calls=%fused_computation.5 | convolution fusion | flops 2434793472 | bytes 44826624 | tf_op jit(solution)/shard_map/stc,snc->tn/dot_general | solution.py:38
  116.2 0.0 reduce-scatter.5.cloned.1.call-update
  116.2 0.0 reduce-scatter.3.cloned.1.call-start
  116.3 0.0 copy-done.1
  116.3 18.9 %multiply_reduce_fusion = f32[768,3072]{1,0:T(8,128)} fusion(f32[4,768,3072]{2,1,0:T(8,128)} %fusion.5, bf16[4,128,768]{2,1,0:T(8,128)(2,1)S(1)} %copy-done, bf16[128,3072]{1,0:T(8,128)(2,1)S(1)} %copy-done.1), kind=kOutput, calls=%fused_computation | convolution fusion | flops 2432434176 | bytes 48758784 | tf_op jit(solution)/shard_map/tn,stc->snc/dot_general | solution.py:46
  135.2 9.0 %multiply_bitcast_fusion = f32[3072,768]{0,1:T(8,128)} fusion(f32[768,3072]{1,0:T(8,128)} %multiply_reduce_fusion), kind=kLoop, calls=%fused_computation.2 | loop fusion | flops 2359296 | bytes 18874368 | tf_op jit(solution)/shard_map/mul | solution.py:48
  144.2 0.0 reduce-scatter.3.cloned.1.call-update
  144.2 16.1 %fusion.4 = bf16[4,128,768]{1,2,0:T(8,128)(2,1)S(1)} fusion(f32[4,768,3072]{2,1,0:T(8,128)} %fusion.5, bf16[3072,768]{0,1:T(8,128)(2,1)} %copy.12, bf16[128,3072]{1,0:T(8,128)(2,1)S(1)} %copy-done.1), kind=kOutput, calls=%fused_computation.7 | convolution fusion | flops 2435186688 | bytes 44040192 | tf_op jit(solution)/shard_map/tn,snc->stc/dot_general | solution.py:32
  160.3 1.2 copy.15
  161.4 0.0 reduce-scatter.5.cloned.1.call-done
  161.4 1.0 convert_element_type.28
  162.5 0.8 copy.17
  163.3 146.9 %reduce-scatter.3.cloned.1.call-done = f32[384,768]{0,1:T(8,128)} async-done(((f32[3072,768]{0,1:T(8,128)}), f32[384,768]{0,1:T(8,128)}) %reduce-scatter.3.cloned.1.call-update) | async-done | bytes 1179664 | tf_op jit(solution)/shard_map/reduce_scatter | solution.py:47
  310.2 2.7 copy.16
  (2 shorter events, 0.0 us)
Async XLA Ops:
  7.2 92.3 %copy-start = (bf16[4,128,768]{2,1,0:T(8,128)(2,1)S(1)}, bf16[4,128,768]{2,1,0:T(8,128)(2,1)}, u32[]{:S(2)}) copy-start(bf16[4,128,768]{2,1,0:T(8,128)(2,1)} %param.7) | copy-start | bytes 2359300
  7.2 85.6 %all-gather.2.cloned.1.call-start = ((), (), s32[]{:S(2)}) async-start(), calls=%async_computation.2 | async-start | bytes 5308416 | tf_op jit(solution)/shard_map/all_gather | solution.py:35
  7.9 153.5 %reduce-scatter.5.cloned.1.call-start = ((), (), s32[]{:S(2)}) async-start(), calls=%async_computation.4 | async-start | bytes 1966080 | tf_op jit(solution)/shard_map/reduce_scatter | solution.py:54
  99.5 16.8 %copy-start.1 = (bf16[128,3072]{1,0:T(8,128)(2,1)S(1)}, bf16[128,3072]{1,0:T(8,128)(2,1)}, u32[]{:S(2)}) copy-start(bf16[128,3072]{1,0:T(8,128)(2,1)} %param.4) | copy-start | bytes 2359300
  116.2 194.0 %reduce-scatter.3.cloned.1.call-start = ((), (), s32[]{:S(2)}) async-start(), calls=%async_computation.3 | async-start | bytes 10616832 | tf_op jit(solution)/shard_map/reduce_scatter | solution.py:47
Sparse Core Ops, SparseCore 0:
  10.2 82.5 all-gather.1
  116.3 26.2 reduce-scatter.4
  146.7 163.4 reduce-scatter.2
where the time goes:
time: 320 us; the launch traced here: 319 us
  waiting for transfers between devices  216 us (68%)
  matrix products  67.2 us (21%)
  between operations  13.8 us (4%)
  local copies, waits for them, and re-layouts  11.3 us (4%)
  other arithmetic  10.8 us (3%)
    reduce_scatter x1, waiting for transfers between devices, on_device(): lax.psum_scatter(jnp.sum(piece_mask(lax.axis_size('dp') * weight.shape[0]...  147 us
    all_gather x1, waiting for transfers between devices, on_device(): lax.all_gather(weight, 'dp', axis=0, tiled=True)  68.6 us
    dot_general x1, matrix products, on_device(): jnp.einsum('tn,stc->snc', cols, out_grad, preferred_element_type=jnp.floa...  18.9 us
    dot_general x1, matrix products, on_device(): jnp.einsum('stc,snc->tn', out_grad, masked_piece(lax.all_gather(weight, '...  16.7 us
    dot_general x1, matrix products, on_device(): jnp.einsum('tn,snc->stc', cols, masked_piece(lax.all_gather(weight, 'dp',...  16.1 us
    dot_general x1, matrix products, piece_mask(): return jnp.einsum('nk,skc->snc', row_select, col_mask)  15.5 us
    mul x1, other arithmetic, on_device(): jnp.sum(piece_mask(lax.axis_size('dp') * weight.shape[0]) * products, axi...  8.99 us
    all_gather x1, local copies, waits for them, and re-layouts, on_device(): lax.all_gather(weight, 'dp', axis=0, tiled=True)  6.65 us
  transfers between devices with their start and end apart: 3, of which 2 were waited for; matrix products, arithmetic and copies ran while one was open for 20% of the time, Pallas kernels for 0%

commit v1 on v0

--- a/solution.py
+++ b/solution.py
@@ -2,9 +2,33 @@
 import jax.numpy as jnp
 from jax import lax
 from jax.sharding import PartitionSpec as P
+from jax.lax import axis_index, ppermute, psum
 
 BS = 256
 TOK_G = 128
+
+
+def keep_up_panel(x_local):
+    reply = psum(1, "dp")
+    s_next = axis_index("dp")
+    mat_out, tile_out, n_now = (reply, s_next, x_local.shape[0])
+    made = [(dev_i, (dev_i + 1) % mat_out) for dev_i in range(mat_out)]
+    lanes = [(dev_i, (dev_i - 1) % mat_out) for dev_i in range(mat_out)]
+    outer = jnp.zeros((*x_local.shape[:0], mat_out * n_now, *x_local.shape[1:]), x_local.dtype)
+    outer = lax.dynamic_update_slice_in_dim(outer, x_local, tile_out * n_now, axis=0)
+    r_now = mat_out // 2
+    local_out = f_next = x_local
+    for to_i in range(1, r_now + 1):
+        local_out = ppermute(local_out, "dp", made)
+        outer = lax.dynamic_update_slice_in_dim(
+            outer, local_out, (tile_out - to_i) % mat_out * n_now, axis=0
+        )
+        if to_i < mat_out - r_now:
+            f_next = ppermute(f_next, "dp", lanes)
+            outer = lax.dynamic_update_slice_in_dim(
+                outer, f_next, (tile_out + to_i) % mat_out * n_now, axis=0
+            )
+    return outer
 
 
 def on_device(acts, weight, block_mask, out_grad):
@@ -30,10 +54,7 @@
 
     cols = acts
     forward = jnp.einsum(
-        "tn,snc->stc",
-        cols,
-        masked_piece(lax.all_gather(weight, "dp", axis=0, tiled=True)),
-        preferred_element_type=jnp.float32,
+        "tn,snc->stc", cols, masked_piece(keep_up_panel(weight)), preferred_element_type=jnp.float32
     )
     input_part = jnp.einsum(
         "stc,snc->tn",

time: 320 us -> 368 us (1.15)
  local copies, waits for them, and re-layouts: 11.3 us -> 29.3 us
  waiting for transfers between devices: 216 us -> 233 us
  starting transfers between devices: 0.12 us -> 13.3 us
    ppermute x0 -> x7, waiting for transfers between devices: none -> 101 us  [the longest x4 86 us: keep_up_panel(): local_out = ppermute(local_out, 'dp', made)]
    reduce_scatter x1, waiting for transfers between devices: 147 us -> 63 us  [on_device(): lax.psum_scatter(jnp.sum(piece_mask(lax.axis_size('dp') * weight.shape[0]...]
    ppermute x0 -> x7, starting transfers between devices: none -> 13.1 us  [the longest x3 10.1 us: keep_up_panel(): f_next = ppermute(f_next, 'dp', lanes)]
    dynamic_update_slice x0 -> x8, local copies, waits for them, and re-layouts: none -> 7.59 us  [the longest x4 3.76 us: keep_up_panel(): lax.dynamic_update_slice_in_dim(outer, local_out, (tile_out - to_i) % mat...]
    ppermute x0 -> x7, local copies, waits for them, and re-layouts: none -> 6.39 us  [the longest x4 3.34 us: keep_up_panel(): local_out = ppermute(local_out, 'dp', made)]
  transfers between devices with their start and end apart: 3 -> 10, of which waited for: 2 -> 9; matrix products, arithmetic and copies ran while one was open for 20% -> 22% of each run, Pallas kernels for 0% -> 0%
where the time goes in v1:
time: 368 us
  waiting for transfers between devices  233 us (63%)
  matrix products  67.2 us (18%)
  local copies, waits for them, and re-layouts  29.3 us (8%)
  between operations  14 us (4%)
  starting transfers between devices  13.3 us (4%)
  other arithmetic  10.8 us (3%)
    ppermute x4, waiting for transfers between devices, keep_up_panel(): local_out = ppermute(local_out, 'dp', made)  86 us
    all_gather x1, waiting for transfers between devices, on_device(): lax.all_gather(weight, 'dp', axis=0, tiled=True)  68.6 us
    reduce_scatter x1, waiting for transfers between devices, on_device(): lax.psum_scatter(jnp.sum(piece_mask(lax.axis_size('dp') * weight.shape[0]...  63 us
    dot_general x1, matrix products, on_device(): jnp.einsum('tn,stc->snc', cols, out_grad, preferred_element_type=jnp.floa...  18.9 us
    dot_general x1, matrix products, on_device(): jnp.einsum('stc,snc->tn', out_grad, masked_piece(lax.all_gather(weight, '...  16.8 us
    dot_general x1, matrix products, on_device(): jnp.einsum('tn,snc->stc', cols, masked_piece(keep_up_panel(weight)), pref...  16 us
    dot_general x1, matrix products, piece_mask(): return jnp.einsum('nk,skc->snc', row_select, col_mask)  15.5 us
    ppermute x3, waiting for transfers between devices, keep_up_panel(): f_next = ppermute(f_next, 'dp', lanes)  15 us
  transfers between devices with their start and end apart: 10, of which 9 were waited for; matrix products, arithmetic and copies ran while one was open for 22% of the time, Pallas kernels for 0%

profile of v1, /device:TPU:0, one launch (start us, length us, event | category | flops | bytes accessed | tf_op | source)
XLA Modules:
  0.0 367.8 jit_solution(496707984934986260)
XLA Ops:
  8.7 15.5 %fusion.9 = f32[4,768,3072]{2,1,0:T(8,128)} fusion(s32[3072]{0:T(1024)S(1)} %add_select_fusion, bf16[4,12,12]{2,0,1:T(4,128)(2,1)S(1)} %convert_element_type.23, s32[768]{0:T(1024)S(1)} %add_select_fusion.1), kind=kOutput, calls=%fused_computation.14 | convolution fusion | flops 227423232 | bytes 37765248 | tf_op jit(solution)/shard_map/nk,skc->snc/dot_general | solution.py:50
  24.2 68.6 %all-gather.2.cloned.1.call-done = bf16[3072,768]{1,0:T(8,128)(2,1)} async-done(((bf16[384,768]{1,0:T(8,128)(2,1)}), bf16[3072,768]{1,0:T(8,128)(2,1)}) %all-gather.2.cloned.1.call-update) | async-done | bytes 4718608 | tf_op jit(solution)/shard_map/all_gather | solution.py:62
  92.8 6.7 %copy.29 = bf16[3072,768]{0,1:T(8,128)(2,1)} copy(bf16[3072,768]{1,0:T(8,128)(2,1)} %all-gather.2.cloned.1.call-done) | data formatting | bytes 9437184 | tf_op jit(solution)/shard_map/all_gather | solution.py:62
  99.5 16.8 %fusion.6 = f32[128,3072]{0,1:T(8,128)} fusion(bf16[4,128,768]{2,1,0:T(8,128)(2,1)S(1)} %copy-done, bf16[3072,768]{0,1:T(8,128)(2,1)} %copy.29, f32[4,768,3072]{2,1,0:T(8,128)} %fusion.9), kind=kOutput, calls=%fused_computation.10 | convolution fusion | flops 2434793472 | bytes 44826624 | tf_op jit(solution)/shard_map/stc,snc->tn/dot_general | solution.py:59
  116.3 18.9 %multiply_reduce_fusion = f32[768,3072]{1,0:T(8,128)} fusion(f32[4,768,3072]{2,1,0:T(8,128)} %fusion.9, bf16[4,128,768]{2,1,0:T(8,128)(2,1)S(1)} %copy-done, bf16[128,3072]{1,0:T(8,128)(2,1)S(1)} %copy-done.2), kind=kOutput, calls=%fused_computation | convolution fusion | flops 2432434176 | bytes 48758784 | tf_op jit(solution)/shard_map/tn,stc->snc/dot_general | solution.py:67
  135.3 9.0 %multiply_bitcast_fusion = f32[3072,768]{0,1:T(8,128)} fusion(f32[768,3072]{1,0:T(8,128)} %multiply_reduce_fusion), kind=kLoop, calls=%fused_computation.6 | loop fusion | flops 2359296 | bytes 18874368 | tf_op jit(solution)/shard_map/mul | solution.py:69
  144.3 1.0 copy-done.3
  145.9 4.2 %collective-permute-start.1 = (bf16[384,768]{1,0:T(8,128)(2,1)S(1)}, bf16[384,768]{1,0:T(8,128)(2,1)}, u32[]{:S(2)}, u32[]{:S(2)}) collective-permute-start(bf16[384,768]{1,0:T(8,128)(2,1)S(1)} %copy-done.3), channel_id=1, source_target_pairs={{0,28},{4,0},{8,4},{12,8},{16,12},{20,16},{24,20},{28,24},{1,29},{... | collective-permute-start | bytes 1769480 | tf_op jit(solution)/shard_map/ppermute | solution.py:27
  150.1 33.9 %collective-permute-done = bf16[384,768]{1,0:T(8,128)(2,1)S(1)} collective-permute-done((bf16[384,768]{1,0:T(8,128)(2,1)S(1)}, bf16[384,768]{1,0:T(8,128)(2,1)S(1)}, u32[]{:S(2)}, u32[]{:S(2)}) %collective-permute-start) | collective-permute-done | bytes 589856 | tf_op jit(solution)/shard_map/ppermute | solution.py:22
  184.0 2.5 collective-permute-start.2
  186.5 2.8 collective-permute-done.1
  189.3 2.9 collective-permute-start.3
  192.2 21.1 %collective-permute-done.2 = bf16[384,768]{1,0:T(8,128)(2,1)} collective-permute-done((bf16[384,768]{1,0:T(8,128)(2,1)S(1)}, bf16[384,768]{1,0:T(8,128)(2,1)}, u32[]{:S(2)}, u32[]{:S(2)}) %collective-permute-start.2) | collective-permute-done | bytes 589856 | tf_op jit(solution)/shard_map/ppermute | solution.py:22
  213.8 6.6 %collective-permute-done.3 = bf16[384,768]{1,0:T(8,128)(2,1)S(1)} collective-permute-done((bf16[384,768]{1,0:T(8,128)(2,1)}, bf16[384,768]{1,0:T(8,128)(2,1)S(1)}, u32[]{:S(2)}, u32[]{:S(2)}) %collective-permute-start.3) | collective-permute-done | bytes 589856 | tf_op jit(solution)/shard_map/ppermute | solution.py:27
  220.4 3.0 collective-permute-start.5
  223.4 2.7 mul.59
  227.3 1.4 copy.22
  228.7 0.9 constant_dynamic-update-slice_fusion.6
  229.6 13.7 %collective-permute-done.4 = bf16[384,768]{1,0:T(8,128)(2,1)S(1)} collective-permute-done((bf16[384,768]{1,0:T(8,128)(2,1)}, bf16[384,768]{1,0:T(8,128)(2,1)S(1)}, u32[]{:S(2)}, u32[]{:S(2)}) %collective-permute-start.4) | collective-permute-done | bytes 589856 | tf_op jit(solution)/shard_map/ppermute | solution.py:22
  243.3 1.1 constant_dynamic-update-slice_fusion.5
  244.4 1.4 copy.23
  246.0 0.9 constant_dynamic-update-slice_fusion.4
  248.2 5.7 %collective-permute-done.5 = bf16[384,768]{1,0:T(8,128)(2,1)} collective-permute-done((bf16[384,768]{1,0:T(8,128)(2,1)S(1)}, bf16[384,768]{1,0:T(8,128)(2,1)}, u32[]{:S(2)}, u32[]{:S(2)}) %collective-permute-start.5) | collective-permute-done | bytes 589856 | tf_op jit(solution)/shard_map/ppermute | solution.py:27
  253.9 1.4 copy.26
  257.1 17.2 %collective-permute-done.6 = bf16[384,768]{1,0:T(8,128)(2,1)} collective-permute-done((bf16[384,768]{1,0:T(8,128)(2,1)S(1)}, bf16[384,768]{1,0:T(8,128)(2,1)}, u32[]{:S(2)}, u32[]{:S(2)}) %collective-permute-start.6) | collective-permute-done | bytes 589856 | tf_op jit(solution)/shard_map/ppermute | solution.py:22
  274.3 1.4 copy.27
  275.7 1.0 constant_dynamic-update-slice_fusion
  276.7 16.0 %fusion.8 = bf16[4,128,768]{1,2,0:T(8,128)(2,1)S(1)} fusion(bf16[3072,768]{0,1:T(8,128)(2,1)} %constant_dynamic-update-slice_fusion, f32[4,768,3072]{2,1,0:T(8,128)} %fusion.9, bf16[128,3072]{1,0:T(8,128)(2,1)S(1)} %copy-done.2), kind=kOutput, calls=%fused_computation.12 | convolution fusion | flops 2435186688 | bytes 44040192 | tf_op jit(solution)/shard_map/tn,snc->stc/dot_general | solution.py:56
  292.6 1.2 copy.31
  293.8 1.0 convert_element_type.28
  295.6 63.0 %reduce-scatter.3.cloned.1.call-done = f32[384,768]{0,1:T(8,128)} async-done(((f32[3072,768]{0,1:T(8,128)}), f32[384,768]{0,1:T(8,128)}) %reduce-scatter.3.cloned.1.call-update) | async-done | bytes 1179664 | tf_op jit(solution)/shard_map/reduce_scatter | solution.py:68
  358.6 2.7 copy.32
  (33 shorter events, 7.9 us)
Async XLA Ops:
  7.2 92.3 %copy-start = (bf16[4,128,768]{2,1,0:T(8,128)(2,1)S(1)}, bf16[4,128,768]{2,1,0:T(8,128)(2,1)}, u32[]{:S(2)}) copy-start(bf16[4,128,768]{2,1,0:T(8,128)(2,1)} %param.7) | copy-start | bytes 2359300
  7.2 85.6 %all-gather.2.cloned.1.call-start = ((), (), s32[]{:S(2)}) async-start(), calls=%async_computation.3 | async-start | bytes 5308416 | tf_op jit(solution)/shard_map/all_gather | solution.py:62
  7.9 285.9 %reduce-scatter.5.cloned.1.call-start = ((), (), s32[]{:S(2)}) async-start(), calls=%async_computation.4 | async-start | bytes 1966080 | tf_op jit(solution)/shard_map/reduce_scatter | solution.py:75
  99.5 16.9 %copy-start.2 = (bf16[128,3072]{1,0:T(8,128)(2,1)S(1)}, bf16[128,3072]{1,0:T(8,128)(2,1)}, u32[]{:S(2)}) copy-start(bf16[128,3072]{1,0:T(8,128)(2,1)} %param.4) | copy-start | bytes 2359300
  116.3 242.3 %reduce-scatter.3.cloned.1.call-start = ((), (), s32[]{:S(2)}) async-start(), calls=%async_computation.2 | async-start | bytes 10616832 | tf_op jit(solution)/shard_map/reduce_scatter | solution.py:68
  144.3 1.1 copy-start.3
  145.4 38.7 %collective-permute-start = (bf16[384,768]{1,0:T(8,128)(2,1)S(1)}, bf16[384,768]{1,0:T(8,128)(2,1)S(1)}, u32[]{:S(2)}, u32[]{:S(2)}) collective-permute-start(bf16[384,768]{1,0:T(8,128)(2,1)S(1)} %copy-done.3), channel_id=1, source_target_pairs={{0,4},{4,8},{8,12},{12,16},{16,20},{20,24},{24,28},{28,0},{1,5},{5... | collective-permute-start | bytes 1769480 | tf_op jit(solution)/shard_map/ppermute | solution.py:22
  145.9 43.4 %collective-permute-start.1 = (bf16[384,768]{1,0:T(8,128)(2,1)S(1)}, bf16[384,768]{1,0:T(8,128)(2,1)}, u32[]{:S(2)}, u32[]{:S(2)}) collective-permute-start(bf16[384,768]{1,0:T(8,128)(2,1)S(1)} %copy-done.3), channel_id=1, source_target_pairs={{0,28},{4,0},{8,4},{12,8},{16,12},{20,16},{24,20},{28,24},{1,29},{... | collective-permute-start | bytes 1769480 | tf_op jit(solution)/shard_map/ppermute | solution.py:27
  184.0 8.2 %copy-start.4 = (bf16[384,768]{1,0:T(8,128)(2,1)}, bf16[384,768]{1,0:T(8,128)(2,1)S(1)}, u32[]{:S(2)}) copy-start(bf16[384,768]{1,0:T(8,128)(2,1)S(1)} %collective-permute-done) | copy-start | bytes 1769476
  184.0 29.3 %collective-permute-start.2 = (bf16[384,768]{1,0:T(8,128)(2,1)S(1)}, bf16[384,768]{1,0:T(8,128)(2,1)}, u32[]{:S(2)}, u32[]{:S(2)}) collective-permute-start(bf16[384,768]{1,0:T(8,128)(2,1)S(1)} %collective-permute-done), channel_id=1, source_target_pairs={{0,4},{4,8},{8,12},{12,16},{16,20},{20,24},{24,28},{28,0},{1,5},{5... | collective-permute-start | bytes 1769480 | tf_op jit(solution)/shard_map/ppermute | solution.py:22
  189.3 31.1 %collective-permute-start.3 = (bf16[384,768]{1,0:T(8,128)(2,1)}, bf16[384,768]{1,0:T(8,128)(2,1)S(1)}, u32[]{:S(2)}, u32[]{:S(2)}) collective-permute-start(bf16[384,768]{1,0:T(8,128)(2,1)} %collective-permute-done.1), channel_id=1, source_target_pairs={{0,28},{4,0},{8,4},{12,8},{16,12},{20,16},{24,20},{28,24},{1,29},{... | collective-permute-start | bytes 1769480 | tf_op jit(solution)/shard_map/ppermute | solution.py:27
  213.3 29.9 %collective-permute-start.4 = (bf16[384,768]{1,0:T(8,128)(2,1)}, bf16[384,768]{1,0:T(8,128)(2,1)S(1)}, u32[]{:S(2)}, u32[]{:S(2)}) collective-permute-start(bf16[384,768]{1,0:T(8,128)(2,1)} %collective-permute-done.2), channel_id=1, source_target_pairs={{0,4},{4,8},{8,12},{12,16},{16,20},{20,24},{24,28},{28,0},{1,5},{5... | collective-permute-start | bytes 1769480 | tf_op jit(solution)/shard_map/ppermute | solution.py:22
  213.7 13.3 %copy-start.5 = (bf16[384,768]{1,0:T(8,128)(2,1)S(1)}, bf16[384,768]{1,0:T(8,128)(2,1)}, u32[]{:S(2)}) copy-start(bf16[384,768]{1,0:T(8,128)(2,1)} %copy-done.4) | copy-start | bytes 1769476
  220.4 33.5 %collective-permute-start.5 = (bf16[384,768]{1,0:T(8,128)(2,1)S(1)}, bf16[384,768]{1,0:T(8,128)(2,1)}, u32[]{:S(2)}, u32[]{:S(2)}) collective-permute-start(bf16[384,768]{1,0:T(8,128)(2,1)S(1)} %collective-permute-done.3), channel_id=1, source_target_pairs={{0,28},{4,0},{8,4},{12,8},{16,12},{20,16},{24,20},{28,24},{1,29},{... | collective-permute-start | bytes 1769480 | tf_op jit(solution)/shard_map/ppermute | solution.py:27
  243.3 31.0 %collective-permute-start.6 = (bf16[384,768]{1,0:T(8,128)(2,1)S(1)}, bf16[384,768]{1,0:T(8,128)(2,1)}, u32[]{:S(2)}, u32[]{:S(2)}) collective-permute-start(bf16[384,768]{1,0:T(8,128)(2,1)S(1)} %collective-permute-done.4), channel_id=1, source_target_pairs={{0,4},{4,8},{8,12},{12,16},{16,20},{20,24},{24,28},{28,0},{1,5},{5... | collective-permute-start | bytes 1769480 | tf_op jit(solution)/shard_map/ppermute | solution.py:22
  276.6 84.6 %copy-start.1 = (bf16[4,128,768]{2,1,0:T(8,128)(2,1)S(1)}, bf16[4,128,768]{2,1,0:T(8,128)(2,1)}, u32[]{:S(2)}) copy-start(bf16[4,128,768]{2,1,0:T(8,128)(2,1)} %param.7) | copy-start | bytes 2359300
Sparse Core Ops, SparseCore 0:
  10.2 82.5 all-gather.1
  116.4 26.2 reduce-scatter.4
  146.8 211.8 reduce-scatter.2
